TPU v7x, 32 devices: a whole 2x2x4 slice. The times are simulated.
32 devices in a mesh: occ: 16 (over z, y, x), grp: 2 (over core).
Axes of the slice: x: 2, y: 2, z: 4, core: 2. Of those that a mesh axis runs over, the one named last changes fastest.
Arguments:
- b_factors: bfloat16 [32, 512, 768], P(('occ', 'grp')), may hold values from -0.29882812 to 0.29882812
- occ_energy: float32 [32], replicated, may hold values from -2 to -0.5
- vir_energy: float32 [512], replicated, may hold values from 0.2 to 3
- integrals: bfloat16 [512, 768, 1024], P('grp', 'occ'), may hold values from -0.0625 to 0.0625
- window_start: int32 [1], replicated, may hold values from 0 to 15
Outputs:
- aux_metric: float32 [768, 768], P('occ', 'grp')
- lagrangian: float32 [32, 1024], P('occ', 'grp')
Inputs may be any that keep to these rules, and one draw needn't show every extreme that they name: `window_start`: the cycle offset of the window's first pair.
All inputs are finite; a program needn't handle non-finite values.
Results may differ from a plain program's by a relative error of at most 0.0034.
Values may be sent and summed in bfloat16 or wider, within the bound.
A program may use at most 128 MiB of HBM per device.

v0:
```python
import functools

import jax
import jax.numpy as jnp
from jax import lax
from jax.experimental import pallas as pl
from jax.experimental.pallas import tpu as pltpu
from jax.sharding import PartitionSpec as P

SHIFTS = 3
MESH = pl.DeviceIdType.MESH


def shifted(x, axis, by):
    size = lax.axis_size(axis)
    return lax.ppermute(x, axis, [(i, (i + by) % size) for i in range(size)])


def pair_kernel(
    n_cycle, chunks,
    own_ref, rot_ref, energy_ref, vir_col_ref, vir_row_ref, dens_out,
    near, far, total, near_ss, near_rs, far_ss, far_rs,
):
    cyc = lax.axis_index("occ")
    grp = lax.axis_index("grp")
    odd = lax.rem(cyc, 2)
    mate = cyc + 1 - 2 * odd
    ahead = lax.rem(cyc + 2, n_cycle)
    behind = lax.rem(cyc + n_cycle - 2, n_cycle)
    size = own_ref.shape[0] // chunks
    barrier = pltpu.get_barrier_semaphore()
    for other in (mate, ahead, behind):
        pl.semaphore_signal(barrier, inc=1, device_id=(other, grp), device_id_type=MESH)
    pl.semaphore_wait(barrier, 3)

    def part(c):
        return pl.ds(c * size, size)

    def far_copy(c):
        return pltpu.make_async_remote_copy(
            src_ref=rot_ref.at[part(c)], dst_ref=far.at[part(c)],
            send_sem=far_ss.at[c], recv_sem=far_rs.at[c],
            device_id=(ahead, grp), device_id_type=MESH,
        )

    def near_copy(c, source):
        return pltpu.make_async_remote_copy(
            src_ref=source.at[part(c)], dst_ref=near.at[part(c)],
            send_sem=near_ss.at[c], recv_sem=near_rs.at[c],
            device_id=(mate, grp), device_id_type=MESH,
        )

    for c in range(chunks):
        far_copy(c).start()

        @pl.when(odd == 0)
        def _():
            near_copy(c, rot_ref).start()

    n_vir = own_ref.shape[0]
    tall = min(256, n_vir)
    across = (((1,), (1,)), ((), ()))

    def term(other, step_no, put):
        @pl.loop(0, n_vir // tall)
        def _(k):
            at = pl.ds(pl.multiple_of(k * tall, tall), tall)
            straight = lax.dot_general(
                own_ref[at, :], other[...], across, preferred_element_type=jnp.float32
            )
            crossed = lax.dot_general(
                other[at, :], own_ref[...], across, preferred_element_type=jnp.float32
            )
            denominator = energy_ref[step_no] - vir_col_ref[at, :] - vir_row_ref[...]
            combined = ((2.0 * straight - crossed) / denominator).astype(jnp.bfloat16)
            put(at, jnp.dot(combined, other[...], preferred_element_type=jnp.float32))

    def put_first(at, value):
        total[at, :] = value

    def put_next(at, value):
        total[at, :] += value

    def put_last(at, value):
        dens_out[at, :] = (total[at, :] + value).astype(dens_out.dtype)

    term(rot_ref, 0, put_first)
    for c in range(chunks):
        far_copy(c).wait_recv()

        @pl.when(odd == 1)
        def _():
            near_copy(c, far).start()

    term(far, 2, put_next)
    for c in range(chunks):
        near_copy(c, rot_ref).wait_recv()
    term(near, 1, put_last)
    for c in range(chunks):
        far_copy(c).wait_send()
        near_copy(c, rot_ref).wait_send()


def pair_densities(n_cycle, own_rows, rotated, energies, vir_energy):
    n_vir, n_aux = own_rows.shape
    chunks = 4
    vmem = pl.BlockSpec(memory_space=pltpu.VMEM)
    dma = pltpu.SemaphoreType.DMA
    block = pltpu.VMEM((n_vir, n_aux), jnp.bfloat16)
    return pl.pallas_call(
        functools.partial(pair_kernel, n_cycle, chunks),
        out_shape=jax.ShapeDtypeStruct((n_vir, n_aux), jnp.bfloat16),
        in_specs=[vmem, vmem, pl.BlockSpec(memory_space=pltpu.SMEM), vmem, vmem],
        out_specs=vmem,
        scratch_shapes=[
            block, block, pltpu.VMEM((n_vir, n_aux), jnp.float32),
            dma((chunks,)), dma((chunks,)), dma((chunks,)), dma((chunks,)),
        ],
        compiler_params=pltpu.CompilerParams(
            collective_id=0, has_side_effects=True, vmem_limit_bytes=40 * 1024 * 1024
        ),
    )(own_rows, rotated, energies, vir_energy[:, None], vir_energy[None, :])


def exchange_kernel(
    n_cycle, n_group, inner, halves, step_cols,
    blocks_ref, dens_ref, own_ref, int_ref, aux_out, lag_out,
    dens_recv, dens_f32, pair_send, pair_recv, aux_sum, plane_send, plane_recv, plane_sum,
    line_send, line_recv, int_vmem, lag_acc, lag_send, lag_recv,
    int_sem, dens_ss, dens_rs, pair_ss, pair_rs, plane_ss, plane_rs, line_ss, line_rs,
    lag_ss, lag_rs,
):
    cyc = lax.axis_index("occ")
    grp = lax.axis_index("grp")
    n_dev = n_cycle * n_group
    me = cyc * n_group + grp
    outer = n_cycle // inner
    seat = lax.rem(cyc, inner)
    plane = cyc // inner
    rows = blocks_ref.shape[1]
    half_rows = rows // halves
    depth = step_cols * 128
    n_steps = rows // step_cols

    def int_copy(k):
        part = pl.ds(pl.multiple_of(k * depth, depth), depth)
        return pltpu.make_async_copy(int_ref.at[part], int_vmem.at[part], int_sem.at[k])

    barrier = pltpu.get_barrier_semaphore()

    @pl.loop(1, n_dev)
    def _(s):
        d = lax.rem(me + s, n_dev)
        pl.semaphore_signal(
            barrier, inc=1, device_id=(d // n_group, lax.rem(d, n_group)), device_id_type=MESH
        )

    @pl.loop(0, n_steps)
    def _(k):
        int_copy(k).start()

    pl.semaphore_wait(barrier, n_dev - 1)

    def dens_copy(h, s):
        d = lax.rem(me + s, n_dev)
        part = pl.ds(h * half_rows, half_rows)
        return pltpu.make_async_remote_copy(
            src_ref=blocks_ref.at[d, part], dst_ref=dens_recv.at[s - 1, part],
            send_sem=dens_ss.at[h, s - 1], recv_sem=dens_rs.at[h, s - 1],
            device_id=(d // n_group, lax.rem(d, n_group)), device_id_type=MESH,
        )

    def pair_copy(s):
        return pltpu.make_async_remote_copy(
            src_ref=pair_send.at[s - 1], dst_ref=pair_recv.at[s - 1],
            send_sem=pair_ss.at[s - 1], recv_sem=pair_rs.at[s - 1],
            device_id=(cyc, lax.rem(grp + s, n_group)), device_id_type=MESH,
        )

    def plane_copy(s):
        q = lax.rem(seat + s, inner)
        return pltpu.make_async_remote_copy(
            src_ref=plane_send.at[s - 1], dst_ref=plane_recv.at[s - 1],
            send_sem=plane_ss.at[s - 1], recv_sem=plane_rs.at[s - 1],
            device_id=(plane * inner + q, grp), device_id_type=MESH,
        )

    def line_copy(s):
        z = lax.rem(plane + s, outer)
        return pltpu.make_async_remote_copy(
            src_ref=line_send.at[s - 1], dst_ref=line_recv.at[s - 1],
            send_sem=line_ss.at[s - 1], recv_sem=line_rs.at[s - 1],
            device_id=(z * inner + seat, grp), device_id_type=MESH,
        )

    def lag_copy(s):
        d = lax.rem(me + s, n_dev)
        return pltpu.make_async_remote_copy(
            src_ref=lag_send.at[d], dst_ref=lag_recv.at[s - 1],
            send_sem=lag_ss.at[s - 1], recv_sem=lag_rs.at[s - 1],
            device_id=(d // n_group, lax.rem(d, n_group)), device_id_type=MESH,
        )

    for h in range(halves):
        @pl.loop(1, n_dev)
        def _(s):
            dens_copy(h, s).start()

    def aux_columns(g):
        return lax.dot_general(
            dens_ref[...], own_ref[g], (((0,), (0,)), ((), ())),
            preferred_element_type=jnp.float32,
        ).reshape(aux_sum.shape)

    for s in range(1, n_group):
        pair_send[s - 1] = aux_columns(lax.rem(grp + s, n_group))
        pair_copy(s).start()
    aux_sum[...] = aux_columns(grp)
    for s in range(1, n_group):
        pair_copy(s).wait_recv()

        @pl.loop(0, n_cycle)
        def _(o):
            aux_sum[o] += pair_recv[s - 1, o]

    for s in range(1, inner):
        q = lax.rem(seat + s, inner)

        @pl.loop(0, outer)
        def _(z):
            plane_send[s - 1, z] = aux_sum[z * inner + q].astype(plane_send.dtype)

        plane_copy(s).start()

    def take_half(h):
        part = pl.ds(h * half_rows, half_rows)
        own_at = pl.ds(me * rows + h * half_rows, half_rows)
        dens_f32[own_at, :] = blocks_ref[me, part].astype(jnp.float32)

        @pl.loop(1, n_dev)
        def _(s):
            dens_copy(h, s).wait_recv()
            source = lax.rem(me - s + n_dev, n_dev)
            at = pl.ds(source * rows + h * half_rows, half_rows)
            dens_f32[at, :] = dens_recv[s - 1, part].astype(jnp.float32)

        steps = n_steps // halves

        @pl.loop(h * steps, (h + 1) * steps)
        def _(k):
            int_copy(k).wait()
            pieces = [
                dens_f32[pl.ds(k * step_cols + j, n_dev, stride=rows), :]
                for j in range(step_cols)
            ]
            left = jnp.concatenate(pieces, axis=1).astype(jnp.bfloat16)
            at = pl.ds(pl.multiple_of(k * depth, depth), depth)
            lag_acc[...] += jnp.dot(left, int_vmem[at, :], preferred_element_type=jnp.float32)

    lag_acc[...] = jnp.zeros_like(lag_acc)
    for h in range(halves - 1):
        take_half(h)

    for s in range(1, inner):
        plane_copy(s).wait_recv()

    @pl.loop(0, outer)
    def _(z):
        block = aux_sum[z * inner + seat]
        for s in range(1, inner):
            block = block + plane_recv[s - 1, z].astype(jnp.float32)
        plane_sum[z] = block

    for s in range(1, outer):
        line_send[s - 1] = plane_sum[lax.rem(plane + s, outer)].astype(line_send.dtype)
        line_copy(s).start()

    take_half(halves - 1)

    orb_block = lag_out.shape[1]
    for o in range(n_cycle):
        for g in range(n_group):
            lag_send[o * n_group + g] = lag_acc[
                o * n_group:(o + 1) * n_group, g * orb_block:(g + 1) * orb_block
            ]

    @pl.loop(1, n_dev)
    def _(s):
        lag_copy(s).start()

    aux_total = plane_sum[plane]
    for s in range(1, outer):
        line_copy(s).wait_recv()
        aux_total = aux_total + line_recv[s - 1].astype(jnp.float32)
    aux_out[...] = aux_total

    lag_out[...] = lag_send[me]

    @pl.loop(1, n_dev)
    def _(s):
        lag_copy(s).wait_recv()
        lag_out[...] += lag_recv[s - 1]

    for s in range(1, n_group):
        pair_copy(s).wait_send()
    for s in range(1, inner):
        plane_copy(s).wait_send()
    for s in range(1, outer):
        line_copy(s).wait_send()

    @pl.loop(1, n_dev)
    def _(s):
        for h in range(halves):
            dens_copy(h, s).wait_send()
        lag_copy(s).wait_send()


def exchange(n_cycle, n_group, dens_blocks, density, own_columns, int_rows):
    n_dev, rows, _ = dens_blocks.shape
    n_vir, n_aux = density.shape
    row_block = n_aux // n_cycle
    col_block = n_aux // n_group
    depth, n_orb = int_rows.shape
    orb_block = n_orb // n_group
    halves = 2 if rows % 32 == 0 else 1
    step_cols = next(c for c in (6, 4, 3, 2, 1) if (rows // halves) % c == 0)
    inner = 4 if n_cycle % 4 == 0 else 1
    outer = n_cycle // inner
    tile = (row_block, col_block)
    vmem = pl.BlockSpec(memory_space=pltpu.VMEM)
    dma = pltpu.SemaphoreType.DMA
    return pl.pallas_call(
        functools.partial(exchange_kernel, n_cycle, n_group, inner, halves, step_cols),
        out_shape=(
            jax.ShapeDtypeStruct(tile, jnp.float32),
            jax.ShapeDtypeStruct((n_group, orb_block), jnp.float32),
        ),
        in_specs=[vmem, vmem, vmem, pl.BlockSpec(memory_space=pl.ANY)],
        out_specs=(vmem, vmem),
        scratch_shapes=[
            pltpu.VMEM((n_dev - 1, rows, 128), jnp.bfloat16),
            pltpu.VMEM((n_dev * rows, 128), jnp.float32),
            pltpu.VMEM((n_group - 1, n_cycle) + tile, jnp.float32),
            pltpu.VMEM((n_group - 1, n_cycle) + tile, jnp.float32),
            pltpu.VMEM((n_cycle,) + tile, jnp.float32),
            pltpu.VMEM((inner - 1, outer) + tile, jnp.bfloat16),
            pltpu.VMEM((inner - 1, outer) + tile, jnp.bfloat16),
            pltpu.VMEM((outer,) + tile, jnp.float32),
            pltpu.VMEM((outer - 1,) + tile, jnp.bfloat16),
            pltpu.VMEM((outer - 1,) + tile, jnp.bfloat16),
            pltpu.VMEM((depth, n_orb), jnp.bfloat16),
            pltpu.VMEM((n_dev, n_orb), jnp.float32),
            pltpu.VMEM((n_dev, n_group, orb_block), jnp.float32),
            pltpu.VMEM((n_dev - 1, n_group, orb_block), jnp.float32),
            dma((rows // step_cols,)),
            dma((halves, n_dev - 1)), dma((halves, n_dev - 1)),
            dma((n_group - 1,)), dma((n_group - 1,)),
            dma((inner - 1,)), dma((inner - 1,)),
            dma((outer - 1,)), dma((outer - 1,)),
            dma((n_dev - 1,)), dma((n_dev - 1,)),
        ],
        compiler_params=pltpu.CompilerParams(
            collective_id=1, has_side_effects=True, vmem_limit_bytes=58 * 1024 * 1024
        ),
    )(dens_blocks, density, own_columns, int_rows)


def local(b_factors, occ_energy, vir_energy, integrals, window_start):
    n_cycle = lax.axis_size("occ")
    n_group = lax.axis_size("grp")
    cycle_pos = lax.axis_index("occ")
    group_pos = lax.axis_index("grp")
    offset = jnp.mod(window_start[0], n_cycle)
    every_orbital = jnp.arange(occ_energy.shape[0], dtype=jnp.int32)
    own_index = cycle_pos * n_group + group_pos
    own_rows = b_factors[0]
    n_vir, n_aux = own_rows.shape
    rotated = lax.switch(
        offset,
        [(lambda x: x)]
        + [functools.partial(lambda by, x: shifted(x, "occ", by), by) for by in range(1, n_cycle)],
        own_rows,
    )
    partners = (
        jnp.mod(cycle_pos - offset - jnp.arange(SHIFTS, dtype=jnp.int32), n_cycle) * n_group
        + group_pos
    )
    own_energy = jnp.sum(jnp.where(every_orbital == own_index, occ_energy, 0.0))
    energies = own_energy + jnp.sum(
        jnp.where(every_orbital[None, :] == partners[:, None], occ_energy[None, :], 0.0), axis=1
    )
    density = pair_densities(n_cycle, own_rows, rotated, energies, vir_energy)
    aux_local = n_aux // n_cycle
    dens_blocks = (
        density.reshape(n_vir, n_cycle, aux_local)
        .transpose(1, 0, 2)
        .reshape(n_cycle * n_group, n_vir // n_group * aux_local // 128, 128)
    )
    own_columns = own_rows.reshape(n_vir, n_group, n_aux // n_group).transpose(1, 0, 2)
    int_rows = integrals.reshape(-1, integrals.shape[2])
    return exchange(n_cycle, n_group, dens_blocks, density, own_columns, int_rows)


def solution(mesh):
    placed = (P(("occ", "grp"), None, None), P(), P(), P("grp", "occ", None), P())
    return jax.shard_map(
        local,
        mesh=mesh,
        in_specs=placed,
        out_specs=(P("occ", "grp"), P("occ", "grp")),
        check_vma=False,
    )
```

profile of v0, /device:TPU:0, one launch (start us, length us, event | category | flops | bytes accessed | tf_op | source)
XLA Modules:
  0.0 107.9 jit_solution(8769315319331654731)
XLA Ops:
  1.3 23.2 %conditional.1 = (bf16[512,768]{1,0:T(8,128)(2,1)}) conditional(s32[]{:T(128)} %clamp.3, bf16[512,768]{1,0:T(8,128)(2,1)} %bitcast.16, bf16[512,768]{1,0:T(8,128)(2,1)} %bitcast.17, bf16[512,768]{1,0:T(8,128)(2,1)} %bitcast.18, bf16[512,768]{1,0:T(8,128)(2,1)} %bitcast.19, bf16[512,768]{1,0:T(8,128)(2,1)} %bitcast.20, ...), branch_computations={%region_0.1_spmd, %region_1.2_spmd, %region_2.3_spmd, %region_3.4_... | conditional | bytes 3145776 | solution.py:378
  1.3 6.1 %collective-permute-start.12 = (bf16[512,768]{1,0:T(8,128)(2,1)}, bf16[512,768]{1,0:T(8,128)(2,1)}, u32[]{:S(2)}, u32[]{:S(2)}) collective-permute-start(bf16[512,768]{1,0:T(8,128)(2,1)} %param.13), channel_id=1, source_target_pairs={{0,26},{2,28},{4,30},{6,0},{8,2},{10,4},{12,6},{14,8},{16,10},{18,... | collective-permute-start | bytes 2359304 | tf_op jit(solution)/shard_map/cond/branch_13_fun/ppermute | solution.py:16
  7.4 17.1 %collective-permute-done.12 = bf16[512,768]{1,0:T(8,128)(2,1)} collective-permute-done((bf16[512,768]{1,0:T(8,128)(2,1)}, bf16[512,768]{1,0:T(8,128)(2,1)}, u32[]{:S(2)}, u32[]{:S(2)}) %collective-permute-start.12) | collective-permute-done | bytes 786464 | tf_op jit(solution)/shard_map/cond/branch_13_fun/ppermute | solution.py:16
  24.5 0.8 select_reduce_fusion
  25.4 1.3 %fusion = f32[]{:T(128)} fusion(f32[32]{0:T(128)} %param.22, s32[]{:T(128)S(6)} %add.34), kind=kLoop, calls=%fused_computation.6 | loop fusion | flops 95 | bytes 136 | tf_op jit(solution)/shard_map/reduce_sum | solution.py:388
  26.6 0.6 broadcast_add_fusion.energy_ref
  27.3 0.8 copy.13.vir_col_ref
  28.1 0.0 copy-start.1
  28.1 0.7 copy-done.1
  28.8 33.3 %shard_map.68.dens_ref = bf16[512,768]{1,0:T(8,128)(2,1)S(1)} custom-call(bf16[512,768]{1,0:T(8,128)(2,1)} %bitcast.32, bf16[512,768]{1,0:T(8,128)(2,1)} %get-tuple-element.39.rot_ref, f32[3]{0:T(128)S(1)} %broadcast_add_fusion.energy_ref, f32[512,1]{1,0:T(8,128)S(1)} %copy.13.vir_col_ref, f32[1,512]{1,0:T(1,128)S(1)} %bitcast.14), custom_call_target="tpu_custom_call" | custom-call | tf_op jit(solution)/shard_map/pallas_call | solution.py:110
  62.1 0.0 copy-start
  62.1 1.2 %copy.14 = bf16[512,768]{0,1:T(8,128)(2,1)} copy(bf16[512,768]{1,0:T(8,128)(2,1)S(1)} %shard_map.68.dens_ref) | data formatting | bytes 1572864 | tf_op jit(solution)/shard_map/pallas_call | solution.py:110
  63.3 2.0 %copy.15 = bf16[16,512,48]{2,1,0:T(8,128)(2,1)S(1)} copy(bf16[16,512,48]{1,2,0:T(8,128)(2,1)} %bitcast.34) | data formatting | bytes 1572864 | tf_op jit(solution)/shard_map/transpose | solution.py:396
  65.3 3.4 %reshape.32.blocks_ref = bf16[32,96,128]{2,1,0:T(8,128)(2,1)} reshape(bf16[16,512,48]{2,1,0:T(8,128)(2,1)S(1)} %copy.15) | data formatting | bytes 1572864 | tf_op jit(solution)/shard_map/reshape | solution.py:397
  68.7 1.4 %copy.16 = bf16[1,512,768]{1,2,0:T(8,128)(2,1)S(1)} copy(bf16[1,512,768]{2,1,0:T(8,128)(2,1)} %param.21) | data formatting | bytes 1572864 | tf_op args[0]
  70.1 1.2 %copy.17 = bf16[512,2,384]{2,0,1:T(8,128)(2,1)} copy(bf16[512,2,384]{0,2,1:T(8,128)(2,1)S(1)} %bitcast.33) | data formatting | bytes 1572864 | tf_op jit(solution)/shard_map/reshape;squeeze | solution.py:399
  71.2 0.0 copy-done
  71.3 33.8 %shard_map.69 = (f32[48,384]{1,0:T(8,128)}, f32[2,512]{1,0:T(2,128)}) custom-call(bf16[32,96,128]{2,1,0:T(8,128)(2,1)} %reshape.32.blocks_ref, bf16[512,768]{1,0:T(8,128)(2,1)} %copy-done, bf16[2,512,384]{2,1,0:T(8,128)(2,1)} %bitcast.35, bf16[12288,1024]{1,0:T(8,128)(2,1)} %bitcast.15), custom_call_target="tpu_custom_call" | custom-call | tf_op jit(solution)/shard_map/pallas_call | solution.py:332
  105.1 1.5 %copy.37 = f32[48,384]{1,0:T(8,128)} copy(f32[48,384]{1,0:T(8,128)} %get-tuple-element.37) | data formatting | bytes 147456
  106.6 1.3 %copy.38 = f32[2,512]{1,0:T(2,128)} copy(f32[2,512]{1,0:T(2,128)} %get-tuple-element.38) | data formatting | bytes 8192
  (1 shorter events, 0.0 us)
Async XLA Ops:
  1.3 23.2 %collective-permute-start.12 = (bf16[512,768]{1,0:T(8,128)(2,1)}, bf16[512,768]{1,0:T(8,128)(2,1)}, u32[]{:S(2)}, u32[]{:S(2)}) collective-permute-start(bf16[512,768]{1,0:T(8,128)(2,1)} %param.13), channel_id=1, source_target_pairs={{0,26},{2,28},{4,30},{6,0},{8,2},{10,4},{12,6},{14,8},{16,10},{18,... | collective-permute-start | bytes 2359304 | tf_op jit(solution)/shard_map/cond/branch_13_fun/ppermute | solution.py:16
  28.1 0.7 copy-start.1
  62.1 9.2 %copy-start = (bf16[512,768]{1,0:T(8,128)(2,1)}, bf16[512,768]{1,0:T(8,128)(2,1)S(1)}, u32[]{:S(2)}) copy-start(bf16[512,768]{1,0:T(8,128)(2,1)S(1)} %shard_map.68.dens_ref) | copy-start | bytes 2359300
where the time goes:
time: 107 us; the launch traced here: 108 us
  Pallas kernels  67.1 us (63%)
  waiting for transfers between devices  17.1 us (16%)
  local copies, waits for them, and re-layouts  13.5 us (13%)
  starting transfers between devices  6.06 us (6%)
  other arithmetic  2.76 us (3%)
  between operations  1.36 us (1%)
    pallas_call x1, Pallas kernels, exchange(): pl.pallas_call(functools.partial(exchange_kernel, n_cycle, n_group, inner...  33.8 us
    pallas_call x1, Pallas kernels, pair_densities(): pl.pallas_call(functools.partial(pair_kernel, n_cycle, chunks), out_shape...  33.3 us
    ppermute x1, waiting for transfers between devices, shifted(): return lax.ppermute(x, axis, [(i, (i + by) % size) for i in range(size)])  17.1 us
    ppermute x1, starting transfers between devices, shifted(): return lax.ppermute(x, axis, [(i, (i + by) % size) for i in range(size)])  6.06 us
    unnamed x7, local copies, waits for them, and re-layouts  4.88 us
    reshape x1, local copies, waits for them, and re-layouts, local(): dens_blocks = density.reshape(n_vir, n_cycle, aux_local).transpose(1, 0,...  3.43 us
  transfers between devices with their start and end apart: 1, of which 1 were waited for; matrix products, arithmetic and copies ran while one was open for 0% of the time, Pallas kernels for 0%

commit v1 on v0

--- a/solution.py
+++ b/solution.py
@@ -1,4 +1,5 @@
 import functools
+import math
 
 import jax
 import jax.numpy as jnp
@@ -7,7 +8,6 @@
 from jax.experimental.pallas import tpu as pltpu
 from jax.sharding import PartitionSpec as P
 
-SHIFTS = 3
 MESH = pl.DeviceIdType.MESH
 
 
@@ -16,10 +16,18 @@
     return lax.ppermute(x, axis, [(i, (i + by) % size) for i in range(size)])
 
 
+def block_plan(n_vir, n_aux, n_cycle, n_group):
+    aux_local, vir_local = n_aux // n_cycle, n_vir // n_group
+    joined = 128 // math.gcd(aux_local, 128)
+    lanes = joined * aux_local // 128
+    halves = 2 if vir_local % (32 * joined) == 0 else 1
+    return aux_local, vir_local, joined, lanes, halves, vir_local // joined // halves
+
+
 def pair_kernel(
-    n_cycle, chunks,
-    own_ref, rot_ref, energy_ref, vir_col_ref, vir_row_ref, dens_out,
-    near, far, total, near_ss, near_rs, far_ss, far_rs,
+    n_cycle, n_group, chunks,
+    own_ref, rot_ref, energy_ref, start_ref, vir_row_ref, dens_out, blocks_out,
+    near, far, total, stage, vir_col_ref, near_ss, near_rs, far_ss, far_rs,
 ):
     cyc = lax.axis_index("occ")
     grp = lax.axis_index("grp")
@@ -57,11 +65,17 @@
         def _():
             near_copy(c, rot_ref).start()
 
-    n_vir = own_ref.shape[0]
+    n_vir, n_aux = own_ref.shape
+    vir_col_ref[...] = jnp.broadcast_to(vir_row_ref[...], (128, n_vir)).T
+    shift = lax.rem(start_ref[0], n_cycle)
+    own_energy = energy_ref[cyc * n_group + grp]
     tall = min(256, n_vir)
     across = (((1,), (1,)), ((), ()))
 
     def term(other, step_no, put):
+        place = lax.rem(cyc - shift - step_no + 2 * n_cycle, n_cycle)
+        energy = own_energy + energy_ref[place * n_group + grp]
+
         @pl.loop(0, n_vir // tall)
         def _(k):
             at = pl.ds(pl.multiple_of(k * tall, tall), tall)
@@ -71,7 +85,7 @@
             crossed = lax.dot_general(
                 other[at, :], own_ref[...], across, preferred_element_type=jnp.float32
             )
-            denominator = energy_ref[step_no] - vir_col_ref[at, :] - vir_row_ref[...]
+            denominator = energy - vir_col_ref[at, 0:1] - vir_row_ref[...]
             combined = ((2.0 * straight - crossed) / denominator).astype(jnp.bfloat16)
             put(at, jnp.dot(combined, other[...], preferred_element_type=jnp.float32))
 
@@ -82,7 +96,10 @@
         total[at, :] += value
 
     def put_last(at, value):
-        dens_out[at, :] = (total[at, :] + value).astype(dens_out.dtype)
+        value = total[at, :] + value
+        for b in range(n_aux // 128):
+            stage[pl.ds(b * n_vir + at.start, tall), :] = value[:, b * 128:(b + 1) * 128]
+        dens_out[at, :] = value.astype(dens_out.dtype)
 
     term(rot_ref, 0, put_first)
     for c in range(chunks):
@@ -96,34 +113,69 @@
     for c in range(chunks):
         near_copy(c, rot_ref).wait_recv()
     term(near, 1, put_last)
+
+    aux_local, vir_local, joined, lanes, halves, tall_block = block_plan(
+        n_vir, n_aux, n_cycle, n_group
+    )
+
+    @pl.loop(0, n_group * halves)
+    def _(k):
+        g, h = k // halves, lax.rem(k, halves)
+        first = k * (tall_block * joined)
+        picked = [
+            jnp.concatenate(
+                [
+                    stage[pl.ds(b * n_vir + first + j, tall_block, stride=joined), :]
+                    for b in range(n_aux // 128)
+                ],
+                axis=1,
+            )
+            for j in range(joined)
+        ]
+        for o in range(n_cycle):
+            wide = jnp.concatenate(
+                [piece[:, o * aux_local:(o + 1) * aux_local] for piece in picked], axis=1
+            ).astype(blocks_out.dtype)
+            for c in range(lanes):
+                blocks_out[o * n_group + g, h * lanes + c] = wide[:, c * 128:(c + 1) * 128]
+
     for c in range(chunks):
         far_copy(c).wait_send()
         near_copy(c, rot_ref).wait_send()
 
 
-def pair_densities(n_cycle, own_rows, rotated, energies, vir_energy):
+def pair_densities(n_cycle, n_group, own_rows, rotated, occ_energy, vir_energy, window_start):
     n_vir, n_aux = own_rows.shape
     chunks = 4
+    _, _, _, lanes, halves, tall_block = block_plan(n_vir, n_aux, n_cycle, n_group)
+    smem = pl.BlockSpec(memory_space=pltpu.SMEM)
     vmem = pl.BlockSpec(memory_space=pltpu.VMEM)
     dma = pltpu.SemaphoreType.DMA
     block = pltpu.VMEM((n_vir, n_aux), jnp.bfloat16)
     return pl.pallas_call(
-        functools.partial(pair_kernel, n_cycle, chunks),
-        out_shape=jax.ShapeDtypeStruct((n_vir, n_aux), jnp.bfloat16),
-        in_specs=[vmem, vmem, pl.BlockSpec(memory_space=pltpu.SMEM), vmem, vmem],
-        out_specs=vmem,
+        functools.partial(pair_kernel, n_cycle, n_group, chunks),
+        out_shape=(
+            jax.ShapeDtypeStruct((n_vir, n_aux), jnp.bfloat16),
+            jax.ShapeDtypeStruct(
+                (n_cycle * n_group, halves * lanes, tall_block, 128), jnp.bfloat16
+            ),
+        ),
+        in_specs=[vmem, vmem, smem, smem, vmem],
+        out_specs=(vmem, vmem),
         scratch_shapes=[
             block, block, pltpu.VMEM((n_vir, n_aux), jnp.float32),
+            pltpu.VMEM((n_aux // 128 * n_vir, 128), jnp.float32),
+            pltpu.VMEM((n_vir, 128), jnp.float32),
             dma((chunks,)), dma((chunks,)), dma((chunks,)), dma((chunks,)),
         ],
         compiler_params=pltpu.CompilerParams(
             collective_id=0, has_side_effects=True, vmem_limit_bytes=40 * 1024 * 1024
         ),
-    )(own_rows, rotated, energies, vir_energy[:, None], vir_energy[None, :])
+    )(own_rows, rotated, occ_energy, window_start, vir_energy[None, :])
 
 
 def exchange_kernel(
-    n_cycle, n_group, inner, halves, step_cols,
+    n_cycle, n_group, inner, halves, lanes, step_rows,
     blocks_ref, dens_ref, own_ref, int_ref, aux_out, lag_out,
     dens_recv, dens_f32, pair_send, pair_recv, aux_sum, plane_send, plane_recv, plane_sum,
     line_send, line_recv, int_vmem, lag_acc, lag_send, lag_recv,
@@ -137,10 +189,11 @@
     outer = n_cycle // inner
     seat = lax.rem(cyc, inner)
     plane = cyc // inner
-    rows = blocks_ref.shape[1]
-    half_rows = rows // halves
-    depth = step_cols * 128
-    n_steps = rows // step_cols
+    tall_block = blocks_ref.shape[2]
+    half_rows = lanes * tall_block
+    rows = halves * half_rows
+    depth = step_rows * lanes * 128
+    n_steps = halves * tall_block // step_rows
 
     def int_copy(k):
         part = pl.ds(pl.multiple_of(k * depth, depth), depth)
@@ -163,7 +216,7 @@
 
     def dens_copy(h, s):
         d = lax.rem(me + s, n_dev)
-        part = pl.ds(h * half_rows, half_rows)
+        part = pl.ds(h * lanes, lanes)
         return pltpu.make_async_remote_copy(
             src_ref=blocks_ref.at[d, part], dst_ref=dens_recv.at[s - 1, part],
             send_sem=dens_ss.at[h, s - 1], recv_sem=dens_rs.at[h, s - 1],
@@ -206,9 +259,15 @@
         def _(s):
             dens_copy(h, s).start()
 
+    def own_part(g):
+        width = aux_out.shape[1]
+        if len(own_ref.shape) == 3:
+            return own_ref[g]
+        return own_ref[:, pl.ds(pl.multiple_of(g * width, 128), width)]
+
     def aux_columns(g):
         return lax.dot_general(
-            dens_ref[...], own_ref[g], (((0,), (0,)), ((), ())),
+            dens_ref[...], own_part(g), (((0,), (0,)), ((), ())),
             preferred_element_type=jnp.float32,
         ).reshape(aux_sum.shape)
 
@@ -233,16 +292,18 @@
         plane_copy(s).start()
 
     def take_half(h):
-        part = pl.ds(h * half_rows, half_rows)
+        part = pl.ds(h * lanes, lanes)
         own_at = pl.ds(me * rows + h * half_rows, half_rows)
-        dens_f32[own_at, :] = blocks_ref[me, part].astype(jnp.float32)
+        own_block = blocks_ref[me, part].astype(jnp.float32)
+        dens_f32[own_at, :] = own_block.reshape(half_rows, 128)
 
         @pl.loop(1, n_dev)
         def _(s):
             dens_copy(h, s).wait_recv()
             source = lax.rem(me - s + n_dev, n_dev)
             at = pl.ds(source * rows + h * half_rows, half_rows)
-            dens_f32[at, :] = dens_recv[s - 1, part].astype(jnp.float32)
+            block = dens_recv[s - 1, part].astype(jnp.float32)
+            dens_f32[at, :] = block.reshape(half_rows, 128)
 
         steps = n_steps // halves
 
@@ -250,8 +311,13 @@
         def _(k):
             int_copy(k).wait()
             pieces = [
-                dens_f32[pl.ds(k * step_cols + j, n_dev, stride=rows), :]
-                for j in range(step_cols)
+                dens_f32[
+                    pl.ds(
+                        h * half_rows + c * tall_block + (k - h * steps) * step_rows + j,
+                        n_dev, stride=rows,
+                    ), :
+                ]
+                for j in range(step_rows) for c in range(lanes)
             ]
             left = jnp.concatenate(pieces, axis=1).astype(jnp.bfloat16)
             at = pl.ds(pl.multiple_of(k * depth, depth), depth)
@@ -316,21 +382,24 @@
 
 
 def exchange(n_cycle, n_group, dens_blocks, density, own_columns, int_rows):
-    n_dev, rows, _ = dens_blocks.shape
+    n_dev = dens_blocks.shape[0]
     n_vir, n_aux = density.shape
     row_block = n_aux // n_cycle
     col_block = n_aux // n_group
     depth, n_orb = int_rows.shape
     orb_block = n_orb // n_group
-    halves = 2 if rows % 32 == 0 else 1
-    step_cols = next(c for c in (6, 4, 3, 2, 1) if (rows // halves) % c == 0)
+    _, _, _, lanes, halves, tall_block = block_plan(n_vir, n_aux, n_cycle, n_group)
+    step_rows = 2 if tall_block % 2 == 0 else 1
+    rows = halves * lanes * tall_block
     inner = 4 if n_cycle % 4 == 0 else 1
     outer = n_cycle // inner
     tile = (row_block, col_block)
     vmem = pl.BlockSpec(memory_space=pltpu.VMEM)
     dma = pltpu.SemaphoreType.DMA
     return pl.pallas_call(
-        functools.partial(exchange_kernel, n_cycle, n_group, inner, halves, step_cols),
+        functools.partial(
+            exchange_kernel, n_cycle, n_group, inner, halves, lanes, step_rows
+        ),
         out_shape=(
             jax.ShapeDtypeStruct(tile, jnp.float32),
             jax.ShapeDtypeStruct((n_group, orb_block), jnp.float32),
@@ -338,7 +407,7 @@
         in_specs=[vmem, vmem, vmem, pl.BlockSpec(memory_space=pl.ANY)],
         out_specs=(vmem, vmem),
         scratch_shapes=[
-            pltpu.VMEM((n_dev - 1, rows, 128), jnp.bfloat16),
+            pltpu.VMEM((n_dev - 1,) + dens_blocks.shape[1:], jnp.bfloat16),
             pltpu.VMEM((n_dev * rows, 128), jnp.float32),
             pltpu.VMEM((n_group - 1, n_cycle) + tile, jnp.float32),
             pltpu.VMEM((n_group - 1, n_cycle) + tile, jnp.float32),
@@ -352,7 +421,7 @@
             pltpu.VMEM((n_dev, n_orb), jnp.float32),
             pltpu.VMEM((n_dev, n_group, orb_block), jnp.float32),
             pltpu.VMEM((n_dev - 1, n_group, orb_block), jnp.float32),
-            dma((rows // step_cols,)),
+            dma((halves * tall_block // step_rows,)),
             dma((halves, n_dev - 1)), dma((halves, n_dev - 1)),
             dma((n_group - 1,)), dma((n_group - 1,)),
             dma((inner - 1,)), dma((inner - 1,)),
@@ -368,11 +437,7 @@
 def local(b_factors, occ_energy, vir_energy, integrals, window_start):
     n_cycle = lax.axis_size("occ")
     n_group = lax.axis_size("grp")
-    cycle_pos = lax.axis_index("occ")
-    group_pos = lax.axis_index("grp")
     offset = jnp.mod(window_start[0], n_cycle)
-    every_orbital = jnp.arange(occ_energy.shape[0], dtype=jnp.int32)
-    own_index = cycle_pos * n_group + group_pos
     own_rows = b_factors[0]
     n_vir, n_aux = own_rows.shape
     rotated = lax.switch(
@@ -381,22 +446,13 @@
         + [functools.partial(lambda by, x: shifted(x, "occ", by), by) for by in range(1, n_cycle)],
         own_rows,
     )
-    partners = (
-        jnp.mod(cycle_pos - offset - jnp.arange(SHIFTS, dtype=jnp.int32), n_cycle) * n_group
-        + group_pos
+    density, dens_blocks = pair_densities(
+        n_cycle, n_group, own_rows, rotated, occ_energy, vir_energy, window_start
     )
-    own_energy = jnp.sum(jnp.where(every_orbital == own_index, occ_energy, 0.0))
-    energies = own_energy + jnp.sum(
-        jnp.where(every_orbital[None, :] == partners[:, None], occ_energy[None, :], 0.0), axis=1
-    )
-    density = pair_densities(n_cycle, own_rows, rotated, energies, vir_energy)
-    aux_local = n_aux // n_cycle
-    dens_blocks = (
-        density.reshape(n_vir, n_cycle, aux_local)
-        .transpose(1, 0, 2)
-        .reshape(n_cycle * n_group, n_vir // n_group * aux_local // 128, 128)
-    )
-    own_columns = own_rows.reshape(n_vir, n_group, n_aux // n_group).transpose(1, 0, 2)
+    col_block = n_aux // n_group
+    own_columns = own_rows
+    if col_block % 128:
+        own_columns = own_rows.reshape(n_vir, n_group, col_block).transpose(1, 0, 2)
     int_rows = integrals.reshape(-1, integrals.shape[2])
     return exchange(n_cycle, n_group, dens_blocks, density, own_columns, int_rows)
 

time: 107 us -> 115 us (1.075); the launches traced: 108 us -> 114 us
  waiting for transfers between devices: 17.1 us -> 34.8 us
  local copies, waits for them, and re-layouts: 13.5 us -> 5.91 us
  other arithmetic: 2.76 us -> 0 us
    ppermute x1, waiting for transfers between devices: 17.1 us -> 34.8 us  [shifted(): return lax.ppermute(x, axis, [(i, (i + by) % size) for i in range(size)])]
    reshape x1 -> x0, local copies, waits for them, and re-layouts: 3.43 us -> none  [local(): dens_blocks = density.reshape(n_vir, n_cycle, aux_local).transpose(1, 0,...]
    reduce_sum x2 -> x0, other arithmetic: 2.1 us -> none  [the longest x1 1.26 us: local(): own_energy = jnp.sum(jnp.where(every_orbital == own_index, occ_energy, 0.0))]
    transpose x1 -> x0, local copies, waits for them, and re-layouts: 1.98 us -> none  [local(): dens_blocks = density.reshape(n_vir, n_cycle, aux_local).transpose(1, 0,...]
    pallas_call x1 -> x0, local copies, waits for them, and re-layouts: 1.2 us -> none  [pair_densities(): pl.pallas_call(functools.partial(pair_kernel, n_cycle, chunks), out_shape...]
    another operation x1 -> x0, local copies, waits for them, and re-layouts: 1.15 us -> none  [local(): own_rows.reshape(n_vir, n_group, n_aux // n_group).transpose(1, 0, 2)]
    unnamed x7 -> x10, local copies, waits for them, and re-layouts: 4.88 us -> 5.91 us
where the time goes in v1:
time: 115 us; the launch traced here: 114 us
  Pallas kernels  67.4 us (59%)
  waiting for transfers between devices  34.8 us (30%)
  local copies, waits for them, and re-layouts  5.91 us (5%)
  starting transfers between devices  4.99 us (4%)
  between operations  1.32 us (1%)
    ppermute x1, waiting for transfers between devices, shifted(): return lax.ppermute(x, axis, [(i, (i + by) % size) for i in range(size)])  34.8 us
    pallas_call x1, Pallas kernels, pair_densities(): pl.pallas_call(functools.partial(pair_kernel, n_cycle, n_group, chunks),...  33.7 us
    pallas_call x1, Pallas kernels, exchange(): pl.pallas_call(functools.partial(exchange_kernel, n_cycle, n_group, inner...  33.7 us
    unnamed x10, local copies, waits for them, and re-layouts  5.91 us
    ppermute x1, starting transfers between devices, shifted(): return lax.ppermute(x, axis, [(i, (i + by) % size) for i in range(size)])  4.99 us
  transfers between devices with their start and end apart: 1, of which 1 were waited for; matrix products, arithmetic and copies ran while one was open for 0% of the time, Pallas kernels for 0%

profile of v1, /device:TPU:0, one launch (start us, length us, event | category | flops | bytes accessed | tf_op | source)
XLA Modules:
  0.0 114.4 jit_solution(1142142035763013883)
XLA Ops:
  1.3 39.8 %conditional.1 = (bf16[512,768]{1,0:T(8,128)(2,1)}) conditional(s32[]{:T(128)} %clamp.3, bf16[512,768]{1,0:T(8,128)(2,1)} %bitcast.9, bf16[512,768]{1,0:T(8,128)(2,1)} %bitcast.10, bf16[512,768]{1,0:T(8,128)(2,1)} %bitcast.11, bf16[512,768]{1,0:T(8,128)(2,1)} %bitcast.12, bf16[512,768]{1,0:T(8,128)(2,1)} %bitcast.13, ...), branch_computations={%region_0.1_spmd, %region_1.2_spmd, %region_2.3_spmd, %region_3.4_... | conditional | bytes 3145776 | solution.py:443
  1.3 5.0 %collective-permute-start.6 = (bf16[512,768]{1,0:T(8,128)(2,1)}, bf16[512,768]{1,0:T(8,128)(2,1)}, u32[]{:S(2)}, u32[]{:S(2)}) collective-permute-start(bf16[512,768]{1,0:T(8,128)(2,1)} %param.7), channel_id=1, source_target_pairs={{0,14},{2,16},{4,18},{6,20},{8,22},{10,24},{12,26},{14,28},{16,30}... | collective-permute-start | bytes 2359304 | tf_op jit(solution)/shard_map/cond/branch_7_fun/ppermute | solution.py:16
  6.3 34.8 %collective-permute-done.6 = bf16[512,768]{1,0:T(8,128)(2,1)} collective-permute-done((bf16[512,768]{1,0:T(8,128)(2,1)}, bf16[512,768]{1,0:T(8,128)(2,1)}, u32[]{:S(2)}, u32[]{:S(2)}) %collective-permute-start.6) | collective-permute-done | bytes 786464 | tf_op jit(solution)/shard_map/cond/branch_7_fun/ppermute | solution.py:16
  41.1 0.0 copy-start.2
  41.1 0.7 copy-done.2
  41.8 0.0 copy-start.3
  41.8 0.7 copy-done.3
  42.4 33.7 %shard_map.68 = (bf16[512,768]{1,0:T(8,128)(2,1)S(1)}, bf16[32,6,16,128]{3,2,1,0:T(8,128)(2,1)S(1)}) custom-call(bf16[512,768]{1,0:T(8,128)(2,1)} %bitcast.25, bf16[512,768]{1,0:T(8,128)(2,1)} %get-tuple-element.43.rot_ref, f32[32]{0:T(128)S(1)} %copy-done.3, s32[1]{0:T(128)} %copy.25.start_ref, f32[1,512]{1,0:T(1,128)S(1)} %bitcast.7), custom_call_target="tpu_custom_call" | custom-call | tf_op jit(solution)/shard_map/pallas_call | solution.py:155
  76.1 0.0 copy-start
  76.2 0.9 copy-done
  77.1 0.0 copy-start.1
  77.1 0.9 copy-done.1
  77.9 33.7 %shard_map.69 = (f32[48,384]{1,0:T(8,128)}, f32[2,512]{1,0:T(2,128)}) custom-call(bf16[32,6,16,128]{3,2,1,0:T(8,128)(2,1)} %copy-done.1, bf16[512,768]{1,0:T(8,128)(2,1)} %copy-done, bf16[512,768]{1,0:T(8,128)(2,1)} %bitcast.26, bf16[12288,1024]{1,0:T(8,128)(2,1)} %bitcast.8), custom_call_target="tpu_custom_call" | custom-call | tf_op jit(solution)/shard_map/pallas_call | solution.py:399
  111.7 1.5 %copy.26 = f32[48,384]{1,0:T(8,128)} copy(f32[48,384]{1,0:T(8,128)} %get-tuple-element.41) | data formatting | bytes 147456
  113.2 1.3 %copy.27 = f32[2,512]{1,0:T(2,128)} copy(f32[2,512]{1,0:T(2,128)} %get-tuple-element.42) | data formatting | bytes 8192
Async XLA Ops:
  1.3 39.8 %collective-permute-start.6 = (bf16[512,768]{1,0:T(8,128)(2,1)}, bf16[512,768]{1,0:T(8,128)(2,1)}, u32[]{:S(2)}, u32[]{:S(2)}) collective-permute-start(bf16[512,768]{1,0:T(8,128)(2,1)} %param.7), channel_id=1, source_target_pairs={{0,14},{2,16},{4,18},{6,20},{8,22},{10,24},{12,26},{14,28},{16,30}... | collective-permute-start | bytes 2359304 | tf_op jit(solution)/shard_map/cond/branch_7_fun/ppermute | solution.py:16
  41.1 0.7 copy-start.2
  41.8 0.7 copy-start.3
  76.1 0.9 copy-start
  77.1 0.9 copy-start.1
